TPU v7x, 32 devices: a whole 2x2x4 slice. The times are simulated.
32 devices in a mesh: py: 4 (over z), px: 2 (over x), pz: 4 (over y, core).
Axes of the slice: x: 2, y: 2, z: 4, core: 2. Of those that a mesh axis runs over, the one named last changes fastest.
Arguments:
- density: float32 [32, 128, 128, 128], P('py', 'px', 'pz'), may hold values from 0.2 to 1.8
- crowding: float32 [32, 128, 128, 128], P('py', 'px', 'pz'), may hold values from 0.5 to 2
Outputs:
- column_sum: float32 [32, 128, 128, 128], P('py', 'px', 'pz')
- density_end: float32 [32, 128, 128, 128], P('py', 'px', 'pz')
All inputs are finite; a program needn't handle non-finite values.
Results may differ from a plain program's by a relative error of at most 0.00002.
Values sent between devices are 32-bit elements; how exact they have to be, the bound alone decides.
A program may use at most 320 MiB of HBM per device.

v0:
```python
import jax
import jax.numpy as jnp
from jax import lax
from jax.sharding import PartitionSpec as P

STEPS = 6


def extended(block, sides, width):
    for axis, dim in sides:
        count = lax.axis_size(axis)
        forward = [(i, i + 1) for i in range(count - 1)]
        backward = [(target, source) for source, target in forward]
        low = lax.ppermute(
            lax.slice_in_dim(block, block.shape[dim] - width, None, axis=dim), axis, forward
        )
        high = lax.ppermute(lax.slice_in_dim(block, 0, width, axis=dim), axis, backward)
        block = jnp.concatenate([low, block, high], axis=dim)
    return block


def entering(part, axis, combine, identity):
    place = lax.axis_index(axis)
    gathered = lax.all_gather(part, axis)
    state = jnp.zeros_like(part) + jnp.asarray(identity, part.dtype)

    def one(turn, state):
        return combine(state, lax.dynamic_index_in_dim(gathered, turn, 0, False))

    return lax.fori_loop(0, place, one, state)


def without_rim(values, dims):
    for dim in dims:
        values = lax.slice_in_dim(values, 1, values.shape[dim] - 1, axis=dim)
    return values


def shifted_cells(values, dim, start, dims):
    others = [other for other in dims if other != dim]
    values = without_rim(values, others)
    return lax.slice_in_dim(values, start, start + values.shape[dim] - 2, axis=dim)


def march_step(padded, crowding):
    middle = without_rim(padded, (0, 1, 2))
    lower = [shifted_cells(padded, dim, 0, (0, 1, 2)) for dim in (0, 1, 2)]
    upper = [shifted_cells(padded, dim, 2, (0, 1, 2)) for dim in (0, 1, 2)]
    spread = lower[0] + upper[0] + lower[1] + upper[1] + lower[2] + upper[2] - 6.0 * middle
    return middle + 0.1 * spread + 0.2 * middle * (1.0 - middle * crowding)


def local(density, crowding):
    for step in range(STEPS):
        padded = extended(density, (("py", 0), ("px", 1), ("pz", 2)), 1)
        density = march_step(padded, crowding)
    here = jnp.cumsum(density, axis=0)
    total = lax.slice_in_dim(here, here.shape[0] - 1, here.shape[0], axis=0)

    def add_pair(earlier_total, later_total):
        return earlier_total + later_total

    below = entering(total, "py", add_pair, jnp.zeros_like(total))
    column_sum = (here + below) / (density.shape[0] * lax.axis_size("py"))
    return (column_sum, density)


def solution(mesh):
    return jax.shard_map(
        local,
        mesh=mesh,
        in_specs=(P("py", "px", "pz", None), P("py", "px", "pz", None)),
        out_specs=(P("py", "px", "pz", None), P("py", "px", "pz", None)),
        check_vma=False,
    )
```

profile of v0, /device:TPU:27, one launch (start us, length us, event | category | flops | bytes accessed | tf_op | source)
XLA Modules:
  0.0 582.3 jit_solution(17351282159391153632)
XLA Ops:
  10.2 4.1 collective-permute-start.1
  14.3 20.6 %collective-permute-done = f32[1,64,32,128]{3,2,1,0:T(8,128)S(1)} collective-permute-done((f32[1,64,32,128]{3,2,1,0:T(8,128)S(1)}, f32[1,64,32,128]{3,2,1,0:T(8,128)S(1)}, u32[]{:S(2)}, u32[]{:S(2)}) %collective-permute-start) | collective-permute-done | bytes 1048608 | tf_op jit(solution)/shard_map/ppermute | solution.py:14
  34.9 4.4 constant_dynamic-update-slice_fusion.1
  41.1 4.5 collective-permute-start.3
  48.4 5.7 collective-permute-start.4
  56.0 2.5 collective-permute-done.4
  58.9 4.1 collective-permute-done.5
  63.3 23.7 %fusion.49 = f32[8,64,32,128]{3,2,1,0:T(8,128)} fusion(f32[8,64,32,128]{3,2,1,0:T(8,128)} %param.4, f32[10,66,1,128]{3,2,1,0:T(1,128)S(1)} %copy.28, f32[10,1,32,128]{3,2,1,0:T(8,128)S(1)} %collective-permute-done.3, f32[10,64,32,128]{3,2,1,0:T(8,128)} %copy-done.5, f32[10,1,32,128]{3,2,1,0:T(8,128)S(1)} %collective-permute-done.2, ...), kind=kLoop, calls=%fused_computation.141 | loop fusion | flops 50331648 | bytes 38752256 | tf_op jit(solution)/shard_map/add | solution.py:50
  90.5 4.1 collective-permute-start.7
  94.5 16.6 %collective-permute-done.6 = f32[1,64,32,128]{3,2,1,0:T(8,128)S(1)} collective-permute-done((f32[1,64,32,128]{3,2,1,0:T(8,128)S(1)}, f32[1,64,32,128]{3,2,1,0:T(8,128)S(1)}, u32[]{:S(2)}, u32[]{:S(2)}) %collective-permute-start.6) | collective-permute-done | bytes 1048608 | tf_op jit(solution)/shard_map/ppermute | solution.py:14
  115.2 4.1 collective-permute-start.9
  122.6 2.2 collective-permute-start.10
  124.9 2.3 collective-permute-start.11
  129.6 4.1 collective-permute-done.11
  134.1 29.2 %fusion.40 = f32[8,64,32,128]{3,2,1,0:T(8,128)} fusion(f32[8,64,32,128]{3,2,1,0:T(8,128)} %fusion.49, f32[10,66,1,128]{3,2,1,0:T(1,128)S(1)} %copy.32, f32[10,1,32,128]{3,2,1,0:T(8,128)} %copy-done.6, f32[10,1,32,128]{3,2,1,0:T(8,128)S(1)} %collective-permute-done.8, f32[1,64,32,128]{3,2,1,0:T(8,128)S(1)} %collective-permute-done.7, ...), kind=kLoop, calls=%fused_computation.114 | loop fusion | flops 67108864 | bytes 28266496 | tf_op jit(solution)/shard_map/add | solution.py:50
  166.7 4.8 collective-permute-start.13
  171.5 16.4 %collective-permute-done.12 = f32[1,64,32,128]{3,2,1,0:T(8,128)S(1)} collective-permute-done((f32[1,64,32,128]{3,2,1,0:T(8,128)S(1)}, f32[1,64,32,128]{3,2,1,0:T(8,128)S(1)}, u32[]{:S(2)}, u32[]{:S(2)}) %collective-permute-start.12) | collective-permute-done | bytes 1048608 | tf_op jit(solution)/shard_map/ppermute | solution.py:14
  191.9 4.1 collective-permute-start.15
  199.3 2.5 collective-permute-start.16
  203.8 2.5 collective-permute-done.16
  206.6 4.1 collective-permute-done.17
  211.0 29.2 %fusion.31 = f32[8,64,32,128]{3,2,1,0:T(8,128)} fusion(f32[8,64,32,128]{3,2,1,0:T(8,128)} %fusion.40, f32[10,66,1,128]{3,2,1,0:T(1,128)S(1)} %copy.36, f32[10,1,32,128]{3,2,1,0:T(8,128)} %copy-done.7, f32[10,1,32,128]{3,2,1,0:T(8,128)S(1)} %collective-permute-done.14, f32[1,64,32,128]{3,2,1,0:T(8,128)S(1)} %collective-permute-done.13, ...), kind=kLoop, calls=%fused_computation.87 | loop fusion | flops 67108864 | bytes 28266496 | tf_op jit(solution)/shard_map/add | solution.py:50
  243.7 4.8 collective-permute-start.19
  248.5 16.4 %collective-permute-done.18 = f32[1,64,32,128]{3,2,1,0:T(8,128)S(1)} collective-permute-done((f32[1,64,32,128]{3,2,1,0:T(8,128)S(1)}, f32[1,64,32,128]{3,2,1,0:T(8,128)S(1)}, u32[]{:S(2)}, u32[]{:S(2)}) %collective-permute-start.18) | collective-permute-done | bytes 1048608 | tf_op jit(solution)/shard_map/ppermute | solution.py:14
  268.9 4.1 collective-permute-start.21
  276.3 2.5 collective-permute-start.22
  281.0 2.3 collective-permute-done.22
  283.6 4.1 collective-permute-done.23
  288.0 29.2 %fusion.22 = f32[8,64,32,128]{3,2,1,0:T(8,128)} fusion(f32[8,64,32,128]{3,2,1,0:T(8,128)} %fusion.31, f32[10,66,1,128]{3,2,1,0:T(1,128)S(1)} %copy.40, f32[10,1,32,128]{3,2,1,0:T(8,128)} %copy-done.8, f32[10,1,32,128]{3,2,1,0:T(8,128)S(1)} %collective-permute-done.20, f32[1,64,32,128]{3,2,1,0:T(8,128)S(1)} %collective-permute-done.19, ...), kind=kLoop, calls=%fused_computation.60 | loop fusion | flops 67108864 | bytes 28266496 | tf_op jit(solution)/shard_map/add | solution.py:50
  320.6 4.8 collective-permute-start.25
  325.4 16.4 %collective-permute-done.24 = f32[1,64,32,128]{3,2,1,0:T(8,128)S(1)} collective-permute-done((f32[1,64,32,128]{3,2,1,0:T(8,128)S(1)}, f32[1,64,32,128]{3,2,1,0:T(8,128)S(1)}, u32[]{:S(2)}, u32[]{:S(2)}) %collective-permute-start.24) | collective-permute-done | bytes 1048608 | tf_op jit(solution)/shard_map/ppermute | solution.py:14
  345.8 4.1 collective-permute-start.27
  353.2 2.5 collective-permute-start.28
  357.7 2.5 collective-permute-done.28
  360.5 4.1 collective-permute-done.29
  364.9 29.2 %fusion.13 = f32[8,64,32,128]{3,2,1,0:T(8,128)} fusion(f32[8,64,32,128]{3,2,1,0:T(8,128)} %fusion.22, f32[10,66,1,128]{3,2,1,0:T(1,128)S(1)} %copy.44, f32[10,1,32,128]{3,2,1,0:T(8,128)} %copy-done.9, f32[10,1,32,128]{3,2,1,0:T(8,128)S(1)} %collective-permute-done.26, f32[1,64,32,128]{3,2,1,0:T(8,128)S(1)} %collective-permute-done.25, ...), kind=kLoop, calls=%fused_computation.33 | loop fusion | flops 67108864 | bytes 28266496 | tf_op jit(solution)/shard_map/add | solution.py:50
  397.6 4.8 collective-permute-start.31
  402.4 16.4 %collective-permute-done.30 = f32[1,64,32,128]{3,2,1,0:T(8,128)S(1)} collective-permute-done((f32[1,64,32,128]{3,2,1,0:T(8,128)S(1)}, f32[1,64,32,128]{3,2,1,0:T(8,128)S(1)}, u32[]{:S(2)}, u32[]{:S(2)}) %collective-permute-start.30) | collective-permute-done | bytes 1048608 | tf_op jit(solution)/shard_map/ppermute | solution.py:14
  422.8 4.1 collective-permute-start.33
  430.2 2.5 collective-permute-start.34
  434.9 2.2 collective-permute-done.34
  437.5 4.1 collective-permute-done.35
  441.9 29.2 %fusion.4 = f32[8,64,32,128]{3,2,1,0:T(8,128)} fusion(f32[8,64,32,128]{3,2,1,0:T(8,128)} %fusion.13, f32[10,66,1,128]{3,2,1,0:T(1,128)S(1)} %copy.48, f32[10,1,32,128]{3,2,1,0:T(8,128)} %copy-done.10, f32[10,1,32,128]{3,2,1,0:T(8,128)S(1)} %collective-permute-done.32, f32[1,64,32,128]{3,2,1,0:T(8,128)S(1)} %collective-permute-done.31, ...), kind=kLoop, calls=%fused_computation.6 | loop fusion | flops 67108864 | bytes 28266496 | tf_op jit(solution)/shard_map/add | solution.py:50
  471.1 7.9 %fusion.61 = f32[8,64,32,128]{3,2,1,0:T(8,128)} fusion(f32[8,64,32,128]{3,2,1,0:T(8,128)} %fusion.4), kind=kOutput, calls=%fused_computation.209 | output fusion | flops 14680064 | bytes 16777216 | tf_op jit(solution)/shard_map/jit(cumsum)/reduce_window_sum | solution.py:57
  479.0 2.3 slice.538
  481.3 80.4 %all-gather.3.cloned.1.call-done = f32[4,64,32,128]{3,2,1,0:T(8,128)} async-done(((f32[1,64,32,128]{3,2,1,0:T(8,128)}), f32[4,64,32,128]{3,2,1,0:T(8,128)}) %all-gather.3.cloned.1.call-update) | async-done | bytes 4194320 | tf_op jit(solution)/shard_map/all_gather | solution.py:24
  561.9 4.6 while.10
  566.5 8.5 %add_multiply_fusion = f32[8,64,32,128]{3,2,1,0:T(8,128)} fusion(f32[8,64,32,128]{3,2,1,0:T(8,128)} %fusion.61, f32[64,32,128]{2,1,0:T(8,128)S(1)} %bitcast.11), kind=kLoop, calls=%fused_computation.155 | loop fusion | flops 4194304 | bytes 17825792 | tf_op jit(solution)/shard_map/div | solution.py:64
  (113 shorter events, 82.2 us)
Async XLA Ops:
  7.2 554.6 %all-gather.3.cloned.1.call-start = ((), (), s32[]{:S(2)}) async-start(), calls=%async_computation | async-start | bytes 5242880 | tf_op jit(solution)/shard_map/all_gather | solution.py:24
  8.9 25.9 %collective-permute-start = (f32[1,64,32,128]{3,2,1,0:T(8,128)S(1)}, f32[1,64,32,128]{3,2,1,0:T(8,128)S(1)}, u32[]{:S(2)}, u32[]{:S(2)}) collective-permute-start(f32[1,64,32,128]{3,2,1,0:T(8,128)S(1)} %get-tuple-element.83), channel_id=1, source_target_pairs={{0,8},{8,16},{16,24},{1,9},{9,17},{17,25},{2,10},{10,18},{18,26},{... | collective-permute-start | bytes 3145736 | tf_op jit(solution)/shard_map/ppermute | solution.py:14
  10.2 29.2 %collective-permute-start.1 = (f32[1,64,32,128]{3,2,1,0:T(8,128)S(1)}, f32[1,64,32,128]{3,2,1,0:T(8,128)S(1)}, u32[]{:S(2)}, u32[]{:S(2)}) collective-permute-start(f32[1,64,32,128]{3,2,1,0:T(8,128)S(1)} %get-tuple-element.82), channel_id=1, source_target_pairs={{8,0},{16,8},{24,16},{9,1},{17,9},{25,17},{10,2},{18,10},{26,18},{... | collective-permute-start | bytes 3145736 | tf_op jit(solution)/shard_map/ppermute | solution.py:17
  39.4 23.9 %slice-start = ((s8[8388608]{0:T(1024)(128)(4,1)}), s8[4194304]{0:T(1024)(128)(4,1)S(1)}, s32[]{:S(2)}) async-start(s8[8388608]{0:T(1024)(128)(4,1)} %bitcast.9), calls=%async_computation.1 | async-start | bytes 8388608
  39.5 8.4 %copy-start.5 = (f32[10,64,32,128]{3,2,1,0:T(8,128)}, f32[10,64,32,128]{3,2,1,0:T(8,128)S(1)}, u32[]{:S(2)}) copy-start(f32[10,64,32,128]{3,2,1,0:T(8,128)S(1)} %constant_dynamic-update-slice_fusion) | copy-start | bytes 31457284
  39.5 6.5 %collective-permute-start.2 = (f32[10,1,32,128]{3,2,1,0:T(8,128)S(1)}, f32[10,1,32,128]{3,2,1,0:T(8,128)S(1)}, u32[]{:S(2)}, u32[]{:S(2)}) collective-permute-start(f32[10,1,32,128]{3,2,1,0:T(8,128)S(1)} %get-tuple-element.70), channel_id=1, source_target_pairs={{0,4},{1,5},{2,6},{3,7},{8,12},{9,13},{10,14},{11,15},{16,20},{17,... | collective-permute-start | bytes 491528 | tf_op jit(solution)/shard_map/ppermute | solution.py:14
  41.1 22.2 %slice-start.1 = ((s8[8388608]{0:T(1024)(128)(4,1)}), s8[4194304]{0:T(1024)(128)(4,1)S(1)}, s32[]{:S(2)}) async-start(s8[8388608]{0:T(1024)(128)(4,1)} %bitcast.9), calls=%async_computation.2 | async-start | bytes 8388608
  41.1 6.8 %collective-permute-start.3 = (f32[10,1,32,128]{3,2,1,0:T(8,128)S(1)}, f32[10,1,32,128]{3,2,1,0:T(8,128)S(1)}, u32[]{:S(2)}, u32[]{:S(2)}) collective-permute-start(f32[10,1,32,128]{3,2,1,0:T(8,128)S(1)} %get-tuple-element.71), channel_id=1, source_target_pairs={{4,0},{5,1},{6,2},{7,3},{12,8},{13,9},{14,10},{15,11},{20,16},{21,... | collective-permute-start | bytes 491528 | tf_op jit(solution)/shard_map/ppermute | solution.py:17
  48.4 10.1 %collective-permute-start.4 = (f32[10,66,1,128]{3,1,2,0:T(8,128)S(1)}, f32[10,66,1,128]{3,1,2,0:T(8,128)S(1)}, u32[]{:S(2)}, u32[]{:S(2)}) collective-permute-start(f32[10,66,1,128]{3,1,2,0:T(8,128)S(1)} %copy.25), channel_id=1, source_target_pairs={{0,1},{1,2},{2,3},{4,5},{5,6},{6,7},{8,9},{9,10},{10,11},{12,13},{... | collective-permute-start | bytes 1013768 | tf_op jit(solution)/shard_map/ppermute | solution.py:14
  54.1 8.8 %collective-permute-start.5 = (f32[10,66,1,128]{3,1,2,0:T(8,128)S(1)}, f32[10,66,1,128]{3,1,2,0:T(8,128)S(1)}, u32[]{:S(2)}, u32[]{:S(2)}) collective-permute-start(f32[10,66,1,128]{3,1,2,0:T(8,128)S(1)} %copy.27), channel_id=1, source_target_pairs={{1,0},{2,1},{3,2},{5,4},{6,5},{7,6},{9,8},{10,9},{11,10},{13,12},{... | collective-permute-start | bytes 1013768 | tf_op jit(solution)/shard_map/ppermute | solution.py:17
  87.0 34.6 %copy-start.4 = (f32[8,64,32,128]{3,2,1,0:T(8,128)S(1)}, f32[8,64,32,128]{3,2,1,0:T(8,128)}, u32[]{:S(2)}) copy-start(f32[8,64,32,128]{3,2,1,0:T(8,128)} %fusion.49) | copy-start | bytes 25165828
  88.9 22.3 %collective-permute-start.6 = (f32[1,64,32,128]{3,2,1,0:T(8,128)S(1)}, f32[1,64,32,128]{3,2,1,0:T(8,128)S(1)}, u32[]{:S(2)}, u32[]{:S(2)}) collective-permute-start(f32[1,64,32,128]{3,2,1,0:T(8,128)S(1)} %get-tuple-element.80), channel_id=1, source_target_pairs={{0,8},{8,16},{16,24},{1,9},{9,17},{17,25},{2,10},{10,18},{18,26},{... | collective-permute-start | bytes 3145736 | tf_op jit(solution)/shard_map/ppermute | solution.py:14
  90.5 22.5 %collective-permute-start.7 = (f32[1,64,32,128]{3,2,1,0:T(8,128)S(1)}, f32[1,64,32,128]{3,2,1,0:T(8,128)S(1)}, u32[]{:S(2)}, u32[]{:S(2)}) collective-permute-start(f32[1,64,32,128]{3,2,1,0:T(8,128)S(1)} %get-tuple-element.81), channel_id=1, source_target_pairs={{8,0},{16,8},{24,16},{9,1},{17,9},{25,17},{10,2},{18,10},{26,18},{... | collective-permute-start | bytes 3145736 | tf_op jit(solution)/shard_map/ppermute | solution.py:17
  113.9 6.2 %collective-permute-start.8 = (f32[10,1,32,128]{3,2,1,0:T(8,128)S(1)}, f32[10,1,32,128]{3,2,1,0:T(8,128)S(1)}, u32[]{:S(2)}, u32[]{:S(2)}) collective-permute-start(f32[10,1,32,128]{3,2,1,0:T(8,128)S(1)} %get-tuple-element.68), channel_id=1, source_target_pairs={{0,4},{1,5},{2,6},{3,7},{8,12},{9,13},{10,14},{11,15},{16,20},{17,... | collective-permute-start | bytes 491528 | tf_op jit(solution)/shard_map/ppermute | solution.py:14
  115.2 6.4 %collective-permute-start.9 = (f32[10,1,32,128]{3,2,1,0:T(8,128)S(1)}, f32[10,1,32,128]{3,2,1,0:T(8,128)S(1)}, u32[]{:S(2)}, u32[]{:S(2)}) collective-permute-start(f32[10,1,32,128]{3,2,1,0:T(8,128)S(1)} %get-tuple-element.69), channel_id=1, source_target_pairs={{4,0},{5,1},{6,2},{7,3},{12,8},{13,9},{14,10},{15,11},{20,16},{21,... | collective-permute-start | bytes 491528 | tf_op jit(solution)/shard_map/ppermute | solution.py:17
  121.6 5.6 copy-start.6
  122.6 6.6 %collective-permute-start.10 = (f32[10,66,1,128]{3,1,2,0:T(8,128)S(1)}, f32[10,66,1,128]{3,1,2,0:T(8,128)S(1)}, u32[]{:S(2)}, u32[]{:S(2)}) collective-permute-start(f32[10,66,1,128]{3,1,2,0:T(8,128)S(1)} %copy.29), channel_id=1, source_target_pairs={{0,1},{1,2},{2,3},{4,5},{5,6},{6,7},{8,9},{9,10},{10,11},{12,13},{... | collective-permute-start | bytes 1013768 | tf_op jit(solution)/shard_map/ppermute | solution.py:14
  124.9 8.8 %collective-permute-start.11 = (f32[10,66,1,128]{3,1,2,0:T(8,128)S(1)}, f32[10,66,1,128]{3,1,2,0:T(8,128)S(1)}, u32[]{:S(2)}, u32[]{:S(2)}) collective-permute-start(f32[10,66,1,128]{3,1,2,0:T(8,128)S(1)} %copy.31), channel_id=1, source_target_pairs={{1,0},{2,1},{3,2},{5,4},{6,5},{7,6},{9,8},{10,9},{11,10},{13,12},{... | collective-permute-start | bytes 1013768 | tf_op jit(solution)/shard_map/ppermute | solution.py:17
  163.2 35.0 %copy-start = (f32[8,64,32,128]{3,2,1,0:T(8,128)S(1)}, f32[8,64,32,128]{3,2,1,0:T(8,128)}, u32[]{:S(2)}) copy-start(f32[8,64,32,128]{3,2,1,0:T(8,128)} %fusion.40) | copy-start | bytes 25165828
  165.1 22.7 %collective-permute-start.12 = (f32[1,64,32,128]{3,2,1,0:T(8,128)S(1)}, f32[1,64,32,128]{3,2,1,0:T(8,128)S(1)}, u32[]{:S(2)}, u32[]{:S(2)}) collective-permute-start(f32[1,64,32,128]{3,2,1,0:T(8,128)S(1)} %get-tuple-element.78), channel_id=1, source_target_pairs={{0,8},{8,16},{16,24},{1,9},{9,17},{17,25},{2,10},{10,18},{18,26},{... | collective-permute-start | bytes 3145736 | tf_op jit(solution)/shard_map/ppermute | solution.py:14
  166.7 22.9 %collective-permute-start.13 = (f32[1,64,32,128]{3,2,1,0:T(8,128)S(1)}, f32[1,64,32,128]{3,2,1,0:T(8,128)S(1)}, u32[]{:S(2)}, u32[]{:S(2)}) collective-permute-start(f32[1,64,32,128]{3,2,1,0:T(8,128)S(1)} %get-tuple-element.79), channel_id=1, source_target_pairs={{8,0},{16,8},{24,16},{9,1},{17,9},{25,17},{10,2},{18,10},{26,18},{... | collective-permute-start | bytes 3145736 | tf_op jit(solution)/shard_map/ppermute | solution.py:17
  190.6 6.2 %collective-permute-start.14 = (f32[10,1,32,128]{3,2,1,0:T(8,128)S(1)}, f32[10,1,32,128]{3,2,1,0:T(8,128)S(1)}, u32[]{:S(2)}, u32[]{:S(2)}) collective-permute-start(f32[10,1,32,128]{3,2,1,0:T(8,128)S(1)} %get-tuple-element.66), channel_id=1, source_target_pairs={{0,4},{1,5},{2,6},{3,7},{8,12},{9,13},{10,14},{11,15},{16,20},{17,... | collective-permute-start | bytes 491528 | tf_op jit(solution)/shard_map/ppermute | solution.py:14
  191.9 6.4 %collective-permute-start.15 = (f32[10,1,32,128]{3,2,1,0:T(8,128)S(1)}, f32[10,1,32,128]{3,2,1,0:T(8,128)S(1)}, u32[]{:S(2)}, u32[]{:S(2)}) collective-permute-start(f32[10,1,32,128]{3,2,1,0:T(8,128)S(1)} %get-tuple-element.67), channel_id=1, source_target_pairs={{4,0},{5,1},{6,2},{7,3},{12,8},{13,9},{14,10},{15,11},{20,16},{21,... | collective-permute-start | bytes 491528 | tf_op jit(solution)/shard_map/ppermute | solution.py:17
  199.3 6.9 %collective-permute-start.16 = (f32[10,66,1,128]{3,1,2,0:T(8,128)S(1)}, f32[10,66,1,128]{3,1,2,0:T(8,128)S(1)}, u32[]{:S(2)}, u32[]{:S(2)}) collective-permute-start(f32[10,66,1,128]{3,1,2,0:T(8,128)S(1)} %copy.33), channel_id=1, source_target_pairs={{0,1},{1,2},{2,3},{4,5},{5,6},{6,7},{8,9},{9,10},{10,11},{12,13},{... | collective-permute-start | bytes 1013768 | tf_op jit(solution)/shard_map/ppermute | solution.py:14
  201.8 8.8 %collective-permute-start.17 = (f32[10,66,1,128]{3,1,2,0:T(8,128)S(1)}, f32[10,66,1,128]{3,1,2,0:T(8,128)S(1)}, u32[]{:S(2)}, u32[]{:S(2)}) collective-permute-start(f32[10,66,1,128]{3,1,2,0:T(8,128)S(1)} %copy.35), channel_id=1, source_target_pairs={{1,0},{2,1},{3,2},{5,4},{6,5},{7,6},{9,8},{10,9},{11,10},{13,12},{... | collective-permute-start | bytes 1013768 | tf_op jit(solution)/shard_map/ppermute | solution.py:17
  240.2 35.0 %copy-start.1 = (f32[8,64,32,128]{3,2,1,0:T(8,128)S(1)}, f32[8,64,32,128]{3,2,1,0:T(8,128)}, u32[]{:S(2)}) copy-start(f32[8,64,32,128]{3,2,1,0:T(8,128)} %fusion.31) | copy-start | bytes 25165828
  242.1 22.7 %collective-permute-start.18 = (f32[1,64,32,128]{3,2,1,0:T(8,128)S(1)}, f32[1,64,32,128]{3,2,1,0:T(8,128)S(1)}, u32[]{:S(2)}, u32[]{:S(2)}) collective-permute-start(f32[1,64,32,128]{3,2,1,0:T(8,128)S(1)} %get-tuple-element.76), channel_id=1, source_target_pairs={{0,8},{8,16},{16,24},{1,9},{9,17},{17,25},{2,10},{10,18},{18,26},{... | collective-permute-start | bytes 3145736 | tf_op jit(solution)/shard_map/ppermute | solution.py:14
  243.7 22.9 %collective-permute-start.19 = (f32[1,64,32,128]{3,2,1,0:T(8,128)S(1)}, f32[1,64,32,128]{3,2,1,0:T(8,128)S(1)}, u32[]{:S(2)}, u32[]{:S(2)}) collective-permute-start(f32[1,64,32,128]{3,2,1,0:T(8,128)S(1)} %get-tuple-element.77), channel_id=1, source_target_pairs={{8,0},{16,8},{24,16},{9,1},{17,9},{25,17},{10,2},{18,10},{26,18},{... | collective-permute-start | bytes 3145736 | tf_op jit(solution)/shard_map/ppermute | solution.py:17
  267.6 6.2 %collective-permute-start.20 = (f32[10,1,32,128]{3,2,1,0:T(8,128)S(1)}, f32[10,1,32,128]{3,2,1,0:T(8,128)S(1)}, u32[]{:S(2)}, u32[]{:S(2)}) collective-permute-start(f32[10,1,32,128]{3,2,1,0:T(8,128)S(1)} %get-tuple-element.64), channel_id=1, source_target_pairs={{0,4},{1,5},{2,6},{3,7},{8,12},{9,13},{10,14},{11,15},{16,20},{17,... | collective-permute-start | bytes 491528 | tf_op jit(solution)/shard_map/ppermute | solution.py:14
  268.9 6.4 %collective-permute-start.21 = (f32[10,1,32,128]{3,2,1,0:T(8,128)S(1)}, f32[10,1,32,128]{3,2,1,0:T(8,128)S(1)}, u32[]{:S(2)}, u32[]{:S(2)}) collective-permute-start(f32[10,1,32,128]{3,2,1,0:T(8,128)S(1)} %get-tuple-element.65), channel_id=1, source_target_pairs={{4,0},{5,1},{6,2},{7,3},{12,8},{13,9},{14,10},{15,11},{20,16},{21,... | collective-permute-start | bytes 491528 | tf_op jit(solution)/shard_map/ppermute | solution.py:17
  275.3 5.7 copy-start.8
  276.3 6.9 %collective-permute-start.22 = (f32[10,66,1,128]{3,1,2,0:T(8,128)S(1)}, f32[10,66,1,128]{3,1,2,0:T(8,128)S(1)}, u32[]{:S(2)}, u32[]{:S(2)}) collective-permute-start(f32[10,66,1,128]{3,1,2,0:T(8,128)S(1)} %copy.37), channel_id=1, source_target_pairs={{0,1},{1,2},{2,3},{4,5},{5,6},{6,7},{8,9},{9,10},{10,11},{12,13},{... | collective-permute-start | bytes 1013768 | tf_op jit(solution)/shard_map/ppermute | solution.py:14
  278.8 8.8 %collective-permute-start.23 = (f32[10,66,1,128]{3,1,2,0:T(8,128)S(1)}, f32[10,66,1,128]{3,1,2,0:T(8,128)S(1)}, u32[]{:S(2)}, u32[]{:S(2)}) collective-permute-start(f32[10,66,1,128]{3,1,2,0:T(8,128)S(1)} %copy.39), channel_id=1, source_target_pairs={{1,0},{2,1},{3,2},{5,4},{6,5},{7,6},{9,8},{10,9},{11,10},{13,12},{... | collective-permute-start | bytes 1013768 | tf_op jit(solution)/shard_map/ppermute | solution.py:17
  317.2 35.0 %copy-start.2 = (f32[8,64,32,128]{3,2,1,0:T(8,128)S(1)}, f32[8,64,32,128]{3,2,1,0:T(8,128)}, u32[]{:S(2)}) copy-start(f32[8,64,32,128]{3,2,1,0:T(8,128)} %fusion.22) | copy-start | bytes 25165828
  319.0 22.7 %collective-permute-start.24 = (f32[1,64,32,128]{3,2,1,0:T(8,128)S(1)}, f32[1,64,32,128]{3,2,1,0:T(8,128)S(1)}, u32[]{:S(2)}, u32[]{:S(2)}) collective-permute-start(f32[1,64,32,128]{3,2,1,0:T(8,128)S(1)} %get-tuple-element.74), channel_id=1, source_target_pairs={{0,8},{8,16},{16,24},{1,9},{9,17},{17,25},{2,10},{10,18},{18,26},{... | collective-permute-start | bytes 3145736 | tf_op jit(solution)/shard_map/ppermute | solution.py:14
  320.6 22.9 %collective-permute-start.25 = (f32[1,64,32,128]{3,2,1,0:T(8,128)S(1)}, f32[1,64,32,128]{3,2,1,0:T(8,128)S(1)}, u32[]{:S(2)}, u32[]{:S(2)}) collective-permute-start(f32[1,64,32,128]{3,2,1,0:T(8,128)S(1)} %get-tuple-element.75), channel_id=1, source_target_pairs={{8,0},{16,8},{24,16},{9,1},{17,9},{25,17},{10,2},{18,10},{26,18},{... | collective-permute-start | bytes 3145736 | tf_op jit(solution)/shard_map/ppermute | solution.py:17
  344.5 6.2 %collective-permute-start.26 = (f32[10,1,32,128]{3,2,1,0:T(8,128)S(1)}, f32[10,1,32,128]{3,2,1,0:T(8,128)S(1)}, u32[]{:S(2)}, u32[]{:S(2)}) collective-permute-start(f32[10,1,32,128]{3,2,1,0:T(8,128)S(1)} %get-tuple-element.62), channel_id=1, source_target_pairs={{0,4},{1,5},{2,6},{3,7},{8,12},{9,13},{10,14},{11,15},{16,20},{17,... | collective-permute-start | bytes 491528 | tf_op jit(solution)/shard_map/ppermute | solution.py:14
  345.8 6.4 %collective-permute-start.27 = (f32[10,1,32,128]{3,2,1,0:T(8,128)S(1)}, f32[10,1,32,128]{3,2,1,0:T(8,128)S(1)}, u32[]{:S(2)}, u32[]{:S(2)}) collective-permute-start(f32[10,1,32,128]{3,2,1,0:T(8,128)S(1)} %get-tuple-element.63), channel_id=1, source_target_pairs={{4,0},{5,1},{6,2},{7,3},{12,8},{13,9},{14,10},{15,11},{20,16},{21,... | collective-permute-start | bytes 491528 | tf_op jit(solution)/shard_map/ppermute | solution.py:17
  353.2 6.9 %collective-permute-start.28 = (f32[10,66,1,128]{3,1,2,0:T(8,128)S(1)}, f32[10,66,1,128]{3,1,2,0:T(8,128)S(1)}, u32[]{:S(2)}, u32[]{:S(2)}) collective-permute-start(f32[10,66,1,128]{3,1,2,0:T(8,128)S(1)} %copy.41), channel_id=1, source_target_pairs={{0,1},{1,2},{2,3},{4,5},{5,6},{6,7},{8,9},{9,10},{10,11},{12,13},{... | collective-permute-start | bytes 1013768 | tf_op jit(solution)/shard_map/ppermute | solution.py:14
  355.8 8.8 %collective-permute-start.29 = (f32[10,66,1,128]{3,1,2,0:T(8,128)S(1)}, f32[10,66,1,128]{3,1,2,0:T(8,128)S(1)}, u32[]{:S(2)}, u32[]{:S(2)}) collective-permute-start(f32[10,66,1,128]{3,1,2,0:T(8,128)S(1)} %copy.43), channel_id=1, source_target_pairs={{1,0},{2,1},{3,2},{5,4},{6,5},{7,6},{9,8},{10,9},{11,10},{13,12},{... | collective-permute-start | bytes 1013768 | tf_op jit(solution)/shard_map/ppermute | solution.py:17
  394.2 35.0 %copy-start.3 = (f32[8,64,32,128]{3,2,1,0:T(8,128)S(1)}, f32[8,64,32,128]{3,2,1,0:T(8,128)}, u32[]{:S(2)}) copy-start(f32[8,64,32,128]{3,2,1,0:T(8,128)} %fusion.13) | copy-start | bytes 25165828
  396.0 22.7 %collective-permute-start.30 = (f32[1,64,32,128]{3,2,1,0:T(8,128)S(1)}, f32[1,64,32,128]{3,2,1,0:T(8,128)S(1)}, u32[]{:S(2)}, u32[]{:S(2)}) collective-permute-start(f32[1,64,32,128]{3,2,1,0:T(8,128)S(1)} %get-tuple-element.72), channel_id=1, source_target_pairs={{0,8},{8,16},{16,24},{1,9},{9,17},{17,25},{2,10},{10,18},{18,26},{... | collective-permute-start | bytes 3145736 | tf_op jit(solution)/shard_map/ppermute | solution.py:14
  397.6 22.9 %collective-permute-start.31 = (f32[1,64,32,128]{3,2,1,0:T(8,128)S(1)}, f32[1,64,32,128]{3,2,1,0:T(8,128)S(1)}, u32[]{:S(2)}, u32[]{:S(2)}) collective-permute-start(f32[1,64,32,128]{3,2,1,0:T(8,128)S(1)} %get-tuple-element.73), channel_id=1, source_target_pairs={{8,0},{16,8},{24,16},{9,1},{17,9},{25,17},{10,2},{18,10},{26,18},{... | collective-permute-start | bytes 3145736 | tf_op jit(solution)/shard_map/ppermute | solution.py:17
  421.5 6.2 %collective-permute-start.32 = (f32[10,1,32,128]{3,2,1,0:T(8,128)S(1)}, f32[10,1,32,128]{3,2,1,0:T(8,128)S(1)}, u32[]{:S(2)}, u32[]{:S(2)}) collective-permute-start(f32[10,1,32,128]{3,2,1,0:T(8,128)S(1)} %get-tuple-element.60), channel_id=1, source_target_pairs={{0,4},{1,5},{2,6},{3,7},{8,12},{9,13},{10,14},{11,15},{16,20},{17,... | collective-permute-start | bytes 491528 | tf_op jit(solution)/shard_map/ppermute | solution.py:14
  422.8 6.4 %collective-permute-start.33 = (f32[10,1,32,128]{3,2,1,0:T(8,128)S(1)}, f32[10,1,32,128]{3,2,1,0:T(8,128)S(1)}, u32[]{:S(2)}, u32[]{:S(2)}) collective-permute-start(f32[10,1,32,128]{3,2,1,0:T(8,128)S(1)} %get-tuple-element.61), channel_id=1, source_target_pairs={{4,0},{5,1},{6,2},{7,3},{12,8},{13,9},{14,10},{15,11},{20,16},{21,... | collective-permute-start | bytes 491528 | tf_op jit(solution)/shard_map/ppermute | solution.py:17
  429.2 5.7 copy-start.10
  430.2 6.9 %collective-permute-start.34 = (f32[10,66,1,128]{3,1,2,0:T(8,128)S(1)}, f32[10,66,1,128]{3,1,2,0:T(8,128)S(1)}, u32[]{:S(2)}, u32[]{:S(2)}) collective-permute-start(f32[10,66,1,128]{3,1,2,0:T(8,128)S(1)} %copy.45), channel_id=1, source_target_pairs={{0,1},{1,2},{2,3},{4,5},{5,6},{6,7},{8,9},{9,10},{10,11},{12,13},{... | collective-permute-start | bytes 1013768 | tf_op jit(solution)/shard_map/ppermute | solution.py:14
  432.8 8.8 %collective-permute-start.35 = (f32[10,66,1,128]{3,1,2,0:T(8,128)S(1)}, f32[10,66,1,128]{3,1,2,0:T(8,128)S(1)}, u32[]{:S(2)}, u32[]{:S(2)}) collective-permute-start(f32[10,66,1,128]{3,1,2,0:T(8,128)S(1)} %copy.47), channel_id=1, source_target_pairs={{1,0},{2,1},{3,2},{5,4},{6,5},{7,6},{9,8},{10,9},{11,10},{13,12},{... | collective-permute-start | bytes 1013768 | tf_op jit(solution)/shard_map/ppermute | solution.py:17
  (2 other events, 11.0 us)
Sparse Core Ops, SparseCore 0:
  481.4 80.2 all-gather.2
where the time goes:
time: 590 us; the launch traced here: 582 us
  waiting for transfers between devices  244 us (41%)
  other arithmetic  201 us (34%)
  starting transfers between devices  99.8 us (17%)
  local copies, waits for them, and re-layouts  22.6 us (4%)
  between operations  15.2 us (3%)
    add x6, other arithmetic, march_step(): return middle + 0.1 * spread + 0.2 * middle * (1.0 - middle * crowding)  170 us
    ppermute x18, waiting for transfers between devices, extended(): lax.ppermute(lax.slice_in_dim(block, block.shape[dim] - width, None, axis...  121 us
    all_gather x1, waiting for transfers between devices, entering(): gathered = lax.all_gather(part, axis)  80.4 us
    ppermute x18, starting transfers between devices, extended(): lax.ppermute(lax.slice_in_dim(block, 0, width, axis=dim), axis, backward)  64.8 us
    ppermute x18, waiting for transfers between devices, extended(): lax.ppermute(lax.slice_in_dim(block, 0, width, axis=dim), axis, backward)  42.6 us
    ppermute x18, starting transfers between devices, extended(): lax.ppermute(lax.slice_in_dim(block, block.shape[dim] - width, None, axis...  34.9 us
  transfers between devices with their start and end apart: 37, of which 36 were waited for; matrix products, arithmetic and copies ran while one was open for 1% of the time, Pallas kernels for 0%

commit v1 on v0

v1 whole, which is shorter than its diff:
```python
import functools

import jax
import jax.numpy as jnp
from jax import lax
from jax.experimental import pallas as pl
from jax.experimental.pallas import tpu as pltpu
from jax.sharding import PartitionSpec as P

STEPS = 6
CHUNKS = 8
AXES = ("py", "px", "pz")
MESH = pl.DeviceIdType.MESH


def kernel(
    counts, chunks, density, crowding, odd, even,
    crowd, y_in, x_in, z_in, z_out, total_in, total_out,
    load_sem, y_send, y_recv, face_send, face_recv, total_send, total_recv,
):
    planes, rows, depth, lanes = density.shape
    part = rows // chunks
    last = planes - 1
    place = [lax.axis_index(axis) for axis in AXES]
    near = []
    for axis, at, count in zip(AXES, place, counts):
        near.append(((at > 0, {axis: at - 1}), (at < count - 1, {axis: at + 1})))
    groups = (pl.ds(0, 1), pl.ds(1, planes - 2), pl.ds(last, 1))

    barrier = pltpu.get_barrier_semaphore()
    awaited = jnp.int32(0)
    for sides in near:
        for there, device in sides:
            awaited = awaited + there.astype(jnp.int32)

            @pl.when(there)
            def _(device=device):
                pl.semaphore_signal(barrier, inc=1, device_id=device, device_id_type=MESH)

    load_field = pltpu.make_async_copy(density, even, load_sem.at[0])
    load_crowd = pltpu.make_async_copy(crowding, crowd, load_sem.at[1])
    load_field.start()
    load_crowd.start()
    pl.semaphore_wait(barrier, awaited)

    def field(level):
        return even if level % 2 == 0 else odd

    def y_copy(level, side, chunk):
        source = density if level == 0 else field(level)
        own = pl.ds(chunk * part, part)
        return pltpu.make_async_remote_copy(
            src_ref=source.at[last if side == 0 else 0, own],
            dst_ref=y_in.at[level, side, own],
            send_sem=y_send.at[level, side, chunk],
            recv_sem=y_recv.at[level, side, chunk],
            device_id=near[0][1 - side][1],
            device_id_type=MESH,
        )

    def face_copy(level, dim, side, group):
        own = groups[group]
        if dim == 1:
            source = density if level == 0 else field(level)
            source, landing = source.at[own, rows - 1 if side == 0 else 0], x_in
        else:
            source, landing = z_out.at[level, side, own], z_in
        slot = (level, (dim - 1) * 2 + side, group)
        return pltpu.make_async_remote_copy(
            src_ref=source,
            dst_ref=landing.at[level, side, own],
            send_sem=face_send.at[slot],
            recv_sem=face_recv.at[slot],
            device_id=near[dim][1 - side][1],
            device_id_type=MESH,
        )

    def total_copy(chunk):
        own = pl.ds(chunk * part, part)
        return pltpu.make_async_remote_copy(
            src_ref=total_out.at[own],
            dst_ref=total_in.at[own],
            send_sem=total_send.at[chunk],
            recv_sem=total_recv.at[chunk],
            device_id=near[0][1][1],
            device_id_type=MESH,
        )

    def sent_to(dim, side):
        return near[dim][1 - side][0]

    def comes_from(dim, side):
        return near[dim][side][0]

    def when(condition, action):
        pl.when(condition)(action)

    def y_start(level, chunk):
        for side in (0, 1):
            when(sent_to(0, side), lambda side=side: y_copy(level, side, chunk).start())

    def y_wait_send(level, chunk):
        for side in (0, 1):
            when(sent_to(0, side), lambda side=side: y_copy(level, side, chunk).wait_send())

    def y_wait_recv(level, chunk):
        for side in (0, 1):
            when(comes_from(0, side), lambda side=side: y_copy(level, side, chunk).wait_recv())

    def faces(level, some, dims, which, act):
        for dim in dims:
            for side in (0, 1):
                def action(dim=dim, side=side):
                    for group in some:
                        getattr(face_copy(level, dim, side, group), act)()

                when(which(dim, side), action)

    OUTER, INNER, ALL = (0, 2), (1,), (0, 2, 1)

    def over(low, high, body):
        lax.fori_loop(low, high, lambda i, carry: (body(i), carry)[1], 0)

    over(0, chunks, lambda chunk: y_start(0, chunk))
    faces(0, ALL, (1,), sent_to, "start")

    for side in (0, 1):
        @pl.when(jnp.logical_not(comes_from(0, side)))
        def _(side=side):
            def clear(row):
                for level in range(STEPS):
                    y_in[level, side, row] = jnp.zeros((depth, lanes), jnp.float32)
            over(0, rows, clear)

        @pl.when(jnp.logical_not(comes_from(1, side)))
        def _(side=side):
            def clear(plane):
                for level in range(STEPS):
                    x_in[level, side, plane] = jnp.zeros((depth, lanes), jnp.float32)
            over(0, planes, clear)

        @pl.when(jnp.logical_not(comes_from(2, side)))
        def _(side=side):
            def clear(plane):
                for level in range(STEPS):
                    z_in[level, side, plane] = jnp.zeros((rows, lanes), jnp.float32)
            over(0, planes, clear)

    load_field.wait()

    def pack(row):
        for plane in range(planes):
            z_out[0, 1, plane, pl.ds(row, 1)] = even[plane, row, 0:1]
            z_out[0, 0, plane, pl.ds(row, 1)] = even[plane, row, depth - 1:depth]

    over(0, rows, pack)
    faces(0, ALL, (2,), sent_to, "start")
    load_crowd.wait()

    index = lax.broadcasted_iota(jnp.int32, (depth, lanes), 0)
    at_low, at_high = index == 0, index == depth - 1

    def advance(level, plane, row, x_edge):
        now = field(level)
        middle = now[plane, row]
        below = y_in[level, 0, row] if plane == 0 else now[plane - 1, row]
        above = y_in[level, 1, row] if plane == last else now[plane + 1, row]
        before = x_in[level, 0, plane] if x_edge < 0 else now[plane, row - 1]
        after = x_in[level, 1, plane] if x_edge > 0 else now[plane, row + 1]
        down = jnp.where(at_low, z_in[level, 0, plane, pl.ds(row, 1)], pltpu.roll(middle, 1, 0))
        up = jnp.where(at_high, z_in[level, 1, plane, pl.ds(row, 1)], pltpu.roll(middle, depth - 1, 0))
        around = ((below + above) + (before + after)) + (down + up)
        rate = 6.0 - 2.0 * (middle * crowd[plane, row])
        value = 0.1 * (around + middle * rate)
        field(level + 1)[plane, row] = value
        if level + 1 < STEPS:
            z_out[level + 1, 1, plane, pl.ds(row, 1)] = value[0:1]
            z_out[level + 1, 0, plane, pl.ds(row, 1)] = value[depth - 1:depth]
        return value

    def sweep(low, high, body):
        when(low == 0, lambda: body(0, -1))
        over(jnp.maximum(low, 1), jnp.minimum(high, rows - 1), lambda row: body(row, 0))
        when(high == rows, lambda: body(rows - 1, 1))

    for level in range(STEPS - 1):
        faces(level, OUTER, (1, 2), comes_from, "wait_recv")
        if level:
            faces(level - 1, OUTER, (1, 2), sent_to, "wait_send")

        def outer(chunk, level=level):
            y_wait_recv(level, chunk)
            if level:
                y_wait_send(level - 1, chunk)

            def cells(row, x_edge):
                for plane in (0, last):
                    advance(level, plane, row, x_edge)

            sweep(chunk * part, (chunk + 1) * part, cells)
            y_start(level + 1, chunk)

        over(0, chunks, outer)
        faces(level + 1, OUTER, (1, 2), sent_to, "start")

        faces(level, INNER, (1, 2), comes_from, "wait_recv")
        if level:
            faces(level - 1, INNER, (1, 2), sent_to, "wait_send")

        def cells(row, x_edge, level=level):
            for plane in range(1, last):
                advance(level, plane, row, x_edge)

        sweep(jnp.int32(0), jnp.int32(rows), cells)
        faces(level + 1, INNER, (1, 2), sent_to, "start")

    final = STEPS - 1
    faces(final, ALL, (1, 2), comes_from, "wait_recv")
    faces(final - 1, ALL, (1, 2), sent_to, "wait_send")
    first, forwards = jnp.logical_not(near[0][0][0]), near[0][1][0]

    def ending(chunk):
        y_wait_recv(final, chunk)
        y_wait_send(final - 1, chunk)

        def cells(row, x_edge):
            total = advance(final, 0, row, x_edge)
            for plane in range(1, planes):
                total = total + advance(final, plane, row, x_edge)
            total_out[row] = total

        sweep(chunk * part, (chunk + 1) * part, cells)
        when(jnp.logical_and(first, forwards), lambda: total_copy(chunk).start())

    over(0, chunks, ending)
    faces(final, ALL, (1, 2), sent_to, "wait_send")
    over(0, chunks, lambda chunk: y_wait_send(final, chunk))

    @pl.when(first)
    def _():
        def clear(row):
            total_in[row] = jnp.zeros((depth, lanes), jnp.float32)
        over(0, rows, clear)

    result, scale = odd, 1.0 / (planes * counts[0])

    def summing(chunk):
        @pl.when(jnp.logical_not(first))
        def _():
            total_copy(chunk).wait_recv()

            @pl.when(forwards)
            def _():
                def add(row):
                    total_out[row] = total_out[row] + total_in[row]
                over(chunk * part, (chunk + 1) * part, add)
                total_copy(chunk).start()

        def cells(row):
            running = total_in[row]
            for plane in range(planes):
                running = running + even[plane, row]
                result[plane, row] = running * scale
        over(chunk * part, (chunk + 1) * part, cells)

    over(0, chunks, summing)
    when(forwards, lambda: over(0, chunks, lambda chunk: total_copy(chunk).wait_send()))


def local(mesh, density, crowding):
    planes, rows, depth, lanes = density.shape
    chunks = CHUNKS if rows % CHUNKS == 0 else 1
    counts = tuple(mesh.shape[axis] for axis in AXES)
    f32 = jnp.float32
    block = (planes, rows, depth, lanes)
    scratch = [
        (block), (STEPS, 2, rows, depth, lanes), (STEPS, 2, planes, depth, lanes),
        (STEPS, 2, planes, rows, lanes), (STEPS, 2, planes, rows, lanes),
        (rows, depth, lanes), (rows, depth, lanes),
    ]
    DMA = pltpu.SemaphoreType.DMA
    cells = planes * rows * depth * lanes
    return pl.pallas_call(
        functools.partial(kernel, counts, chunks),
        out_shape=(pltpu.VMEM(block, f32), pltpu.VMEM(block, f32)),
        in_specs=[pl.BlockSpec(memory_space=pltpu.HBM)] * 2,
        out_specs=(pl.BlockSpec(memory_space=pltpu.VMEM), pl.BlockSpec(memory_space=pltpu.VMEM)),
        scratch_shapes=[pltpu.VMEM(shape, f32) for shape in scratch] + [
            DMA((2,)),
            DMA((STEPS, 2, chunks)), DMA((STEPS, 2, chunks)),
            DMA((STEPS, 4, 3)), DMA((STEPS, 4, 3)),
            DMA((chunks,)), DMA((chunks,)),
        ],
        compiler_params=pltpu.CompilerParams(
            collective_id=0, has_side_effects=True, vmem_limit_bytes=40 * 2**20
        ),
        cost_estimate=pl.CostEstimate(flops=cells * 66, bytes_accessed=cells * 16, transcendentals=0),
        name="march",
    )(density, crowding)


def solution(mesh):
    spec = P(*AXES, None)
    return jax.shard_map(
        functools.partial(local, mesh), mesh=mesh, in_specs=(spec, spec), out_specs=(spec, spec), check_vma=False
    )
```

time: 590 us -> 180 us (0.31); the launches traced: 582 us -> 178 us
  waiting for transfers between devices: 244 us -> 0 us
  other arithmetic: 201 us -> 0 us
  Pallas kernels: 0 us -> 171 us
  starting transfers between devices: 99.8 us -> 0 us
  local copies, waits for them, and re-layouts: 22.6 us -> 6.8 us
  between operations: 15.2 us -> 0.64 us
    add x9 -> x0, other arithmetic: 174 us -> none  [the longest x6 170 us: march_step(): return middle + 0.1 * spread + 0.2 * middle * (1.0 - middle * crowding)]
    pallas_call x0 -> x1, Pallas kernels: none -> 171 us  [local(): pl.pallas_call(functools.partial(kernel, counts, chunks), out_shape=(pltp...]
    ppermute x36 -> x0, waiting for transfers between devices: 163 us -> none  [the longest x18 121 us: extended(): lax.ppermute(lax.slice_in_dim(block, block.shape[dim] - width, None, axis...]
    ppermute x36 -> x0, starting transfers between devices: 99.7 us -> none  [the longest x18 64.8 us: extended(): lax.ppermute(lax.slice_in_dim(block, 0, width, axis=dim), axis, backward)]
    all_gather x1 -> x0, waiting for transfers between devices: 80.4 us -> none  [entering(): gathered = lax.all_gather(part, axis)]
    slice x20 -> x0, local copies, waits for them, and re-layouts: 13.7 us -> none  [the longest x12 9.5 us: extended(): lax.slice_in_dim(block, block.shape[dim] - width, None, axis=dim)]
    slice x11 -> x0, other arithmetic: 10.4 us -> none  [extended(): lax.slice_in_dim(block, block.shape[dim] - width, None, axis=dim)]
    div x1 -> x0, other arithmetic: 8.49 us -> none  [local(): column_sum = (here + below) / (density.shape[0] * lax.axis_size('py'))]
  transfers between devices with their start and end apart: 37 -> 0, of which waited for: 36 -> 0; matrix products, arithmetic and copies ran while one was open for 1% -> 0% of each run, Pallas kernels for 0% -> 0%
where the time goes in v1:
time: 180 us; the launch traced here: 178 us
  Pallas kernels  171 us (95%)
  local copies, waits for them, and re-layouts  6.8 us (4%)
    pallas_call x1, Pallas kernels, local(): pl.pallas_call(functools.partial(kernel, counts, chunks), out_shape=(pltp...  171 us
    unnamed x2, local copies, waits for them, and re-layouts  6.8 us

profile of v1, /device:TPU:27, one launch (start us, length us, event | category | flops | bytes accessed | tf_op | source)
XLA Modules:
  0.0 178.3 jit_solution(3639238449443795671)
XLA Ops:
  0.6 170.9 %march.1 = (f32[8,64,32,128]{3,2,1,0:T(8,128)S(1)}, f32[8,64,32,128]{3,2,1,0:T(8,128)S(1)}) custom-call(f32[8,64,32,128]{3,2,1,0:T(8,128)} %density.1, f32[8,64,32,128]{3,2,1,0:T(8,128)} %crowding.1), custom_call_target="tpu_custom_call" | custom-call | flops 138412032 | bytes 33554432 | tf_op jit(solution)/shard_map/march/pallas_call | solution.py:283
  171.5 3.4 %copy.6 = f32[8,64,32,128]{3,2,1,0:T(8,128)} copy(f32[8,64,32,128]{3,2,1,0:T(8,128)S(1)} %get-tuple-element.2) | data formatting | bytes 16777216
  174.9 3.4 %copy.7 = f32[8,64,32,128]{3,2,1,0:T(8,128)} copy(f32[8,64,32,128]{3,2,1,0:T(8,128)S(1)} %get-tuple-element.3) | data formatting | bytes 16777216

commit v2 on v1

--- a/solution.py
+++ b/solution.py
@@ -9,17 +9,19 @@
 
 STEPS = 6
 CHUNKS = 8
+PIECES = 4
 AXES = ("py", "px", "pz")
 MESH = pl.DeviceIdType.MESH
 
 
 def kernel(
-    counts, chunks, density, crowding, odd, even,
+    counts, chunks, pieces, density, crowding, odd, even,
     crowd, y_in, x_in, z_in, z_out, total_in, total_out,
     load_sem, y_send, y_recv, face_send, face_recv, total_send, total_recv,
 ):
     planes, rows, depth, lanes = density.shape
     part = rows // chunks
+    bit = part // pieces
     last = planes - 1
     place = [lax.axis_index(axis) for axis in AXES]
     near = []
@@ -75,13 +77,13 @@
             device_id_type=MESH,
         )
 
-    def total_copy(chunk):
-        own = pl.ds(chunk * part, part)
+    def total_copy(piece):
+        own = pl.ds(piece * bit, bit)
         return pltpu.make_async_remote_copy(
             src_ref=total_out.at[own],
             dst_ref=total_in.at[own],
-            send_sem=total_send.at[chunk],
-            recv_sem=total_recv.at[chunk],
+            send_sem=total_send.at[piece],
+            recv_sem=total_recv.at[piece],
             device_id=near[0][1][1],
             device_id_type=MESH,
         )
@@ -230,7 +232,9 @@
             total_out[row] = total
 
         sweep(chunk * part, (chunk + 1) * part, cells)
-        when(jnp.logical_and(first, forwards), lambda: total_copy(chunk).start())
+        when(jnp.logical_and(first, forwards), lambda: over(
+            chunk * pieces, (chunk + 1) * pieces, lambda piece: total_copy(piece).start()
+        ))
 
     over(0, chunks, ending)
     faces(final, ALL, (1, 2), sent_to, "wait_send")
@@ -244,32 +248,46 @@
 
     result, scale = odd, 1.0 / (planes * counts[0])
 
-    def summing(chunk):
+    def summing(piece):
+        low, high = piece * bit, (piece + 1) * bit
+
         @pl.when(jnp.logical_not(first))
         def _():
-            total_copy(chunk).wait_recv()
+            total_copy(piece).wait_recv()
 
             @pl.when(forwards)
             def _():
                 def add(row):
                     total_out[row] = total_out[row] + total_in[row]
-                over(chunk * part, (chunk + 1) * part, add)
-                total_copy(chunk).start()
+                over(low, high, add)
+                total_copy(piece).start()
 
         def cells(row):
             running = total_in[row]
             for plane in range(planes):
                 running = running + even[plane, row]
                 result[plane, row] = running * scale
-        over(chunk * part, (chunk + 1) * part, cells)
-
-    over(0, chunks, summing)
-    when(forwards, lambda: over(0, chunks, lambda chunk: total_copy(chunk).wait_send()))
+        over(low, high, cells)
+
+    over(0, chunks * pieces, summing)
+    when(forwards, lambda: over(0, chunks * pieces, lambda piece: total_copy(piece).wait_send()))
+
+
+def store(sums, field, column_sum, density_end, sem):
+    planes = sums.shape[0]
+    copies = []
+    for plane in range(planes):
+        for source, target in ((field, density_end), (sums, column_sum)):
+            copies.append(pltpu.make_async_copy(source.at[plane], target.at[plane], sem.at[len(copies)]))
+            copies[-1].start()
+    for copy in copies:
+        copy.wait()
 
 
 def local(mesh, density, crowding):
     planes, rows, depth, lanes = density.shape
     chunks = CHUNKS if rows % CHUNKS == 0 else 1
+    pieces = PIECES if (rows // chunks) % PIECES == 0 else 1
     counts = tuple(mesh.shape[axis] for axis in AXES)
     f32 = jnp.float32
     block = (planes, rows, depth, lanes)
@@ -280,8 +298,8 @@
     ]
     DMA = pltpu.SemaphoreType.DMA
     cells = planes * rows * depth * lanes
-    return pl.pallas_call(
-        functools.partial(kernel, counts, chunks),
+    sums, field = pl.pallas_call(
+        functools.partial(kernel, counts, chunks, pieces),
         out_shape=(pltpu.VMEM(block, f32), pltpu.VMEM(block, f32)),
         in_specs=[pl.BlockSpec(memory_space=pltpu.HBM)] * 2,
         out_specs=(pl.BlockSpec(memory_space=pltpu.VMEM), pl.BlockSpec(memory_space=pltpu.VMEM)),
@@ -289,7 +307,7 @@
             DMA((2,)),
             DMA((STEPS, 2, chunks)), DMA((STEPS, 2, chunks)),
             DMA((STEPS, 4, 3)), DMA((STEPS, 4, 3)),
-            DMA((chunks,)), DMA((chunks,)),
+            DMA((chunks * pieces,)), DMA((chunks * pieces,)),
         ],
         compiler_params=pltpu.CompilerParams(
             collective_id=0, has_side_effects=True, vmem_limit_bytes=40 * 2**20
@@ -297,6 +315,16 @@
         cost_estimate=pl.CostEstimate(flops=cells * 66, bytes_accessed=cells * 16, transcendentals=0),
         name="march",
     )(density, crowding)
+    return pl.pallas_call(
+        store,
+        out_shape=(jax.ShapeDtypeStruct(block, f32), jax.ShapeDtypeStruct(block, f32)),
+        in_specs=[pl.BlockSpec(memory_space=pltpu.VMEM)] * 2,
+        out_specs=(pl.BlockSpec(memory_space=pltpu.HBM), pl.BlockSpec(memory_space=pltpu.HBM)),
+        scratch_shapes=[DMA((2 * planes,))],
+        compiler_params=pltpu.CompilerParams(vmem_limit_bytes=2**20),
+        cost_estimate=pl.CostEstimate(flops=0, bytes_accessed=cells * 8, transcendentals=0),
+        name="store",
+    )(sums, field)
 
 
 def solution(mesh):

time: 180 us -> 176 us (0.978)
  local copies, waits for them, and re-layouts: 6.8 us -> 0 us
  Pallas kernels: 171 us -> 174 us
    unnamed x2 -> x0, local copies, waits for them, and re-layouts: 6.8 us -> none
    pallas_call x1 -> x2, Pallas kernels: 171 us -> 174 us  [the longest x1 168 us: local(): pl.pallas_call(functools.partial(kernel, counts, chunks, pieces), out_sha...]
where the time goes in v2:
time: 176 us; the launch traced here: 175 us
  Pallas kernels  174 us (99%)
    pallas_call x1, Pallas kernels, local(): pl.pallas_call(functools.partial(kernel, counts, chunks, pieces), out_sha...  168 us
    pallas_call x1, Pallas kernels, local(): pl.pallas_call(store, out_shape=(jax.ShapeDtypeStruct(block, f32), jax.Sh...  5.96 us

profile of v2, /device:TPU:27, one launch (start us, length us, event | category | flops | bytes accessed | tf_op | source)
XLA Modules:
  0.0 174.5 jit_solution(9975217854341971089)
XLA Ops:
  0.6 167.9 %march.1 = (f32[8,64,32,128]{3,2,1,0:T(8,128)S(1)}, f32[8,64,32,128]{3,2,1,0:T(8,128)S(1)}) custom-call(f32[8,64,32,128]{3,2,1,0:T(8,128)} %density.1, f32[8,64,32,128]{3,2,1,0:T(8,128)} %crowding.1), custom_call_target="tpu_custom_call" | custom-call | flops 138412032 | bytes 33554432 | tf_op jit(solution)/shard_map/march/pallas_call | solution.py:301
  168.6 6.0 %store.1 = (f32[8,64,32,128]{3,2,1,0:T(8,128)}, f32[8,64,32,128]{3,2,1,0:T(8,128)}) custom-call(f32[8,64,32,128]{3,2,1,0:T(8,128)S(1)} %get-tuple-element.4.sums, f32[8,64,32,128]{3,2,1,0:T(8,128)S(1)} %get-tuple-element.5.field), custom_call_target="tpu_custom_call" | custom-call | bytes 16777216 | tf_op jit(solution)/shard_map/store/pallas_call | solution.py:318
